TPU v7x, 512 devices: a whole 4x4x16 slice. The times are simulated.
512 devices in a mesh: dp: 32 (over x, y, core), expert: 16 (over z).
Axes of the slice: x: 4, y: 4, z: 16, core: 2. Of those that a mesh axis runs over, the one named last changes fastest.
Arguments:
- tokens: bfloat16 [4096, 2048], P('dp', 'expert'), may hold values from -6 to 6
- cotangent: bfloat16 [4096, 2048], P('dp', 'expert'), may hold values from -6 to 6
- expert_ids: int32 [4096, 8], P('dp'), may hold values from 0 to 127, all different within a row; in each aligned block of 128 rows (0 to 127, 128 to 255, ...) at most 16 rows name the same one
- gate_weights: float32 [4096, 8], P('dp'), may hold values from 0.05 to 1
- w_gate: bfloat16 [512, 192, 2048], P(('dp', 'expert')), may hold values from -0.125 to 0.125
- w_up: bfloat16 [512, 192, 2048], P(('dp', 'expert')), may hold values from -0.125 to 0.125
- w_down: bfloat16 [512, 192, 2048], P(('dp', 'expert')), may hold values from -0.21875 to 0.21875
Outputs:
- layer_out: bfloat16 [4096, 2048], P('dp', 'expert')
- grad_tokens: bfloat16 [4096, 2048], P('dp', 'expert')
- grad_gates: float32 [4096, 8], P('dp')
- grad_w_gate: bfloat16 [512, 192, 2048], P(('dp', 'expert'))
- grad_w_up: bfloat16 [512, 192, 2048], P(('dp', 'expert'))
- grad_w_down: bfloat16 [512, 192, 2048], P(('dp', 'expert'))
Inputs may be any that keep to these rules, and one draw needn't show every extreme that they name: `expert_ids`: each row names 8 different experts. In each aligned block of 128 rows (the rows of one index of dp) no expert is named by more than 16 rows, and in some block an expert is named by exactly 16 rows.
All inputs are finite; a program needn't handle non-finite values.
Results may differ from a plain program's by a relative error of at most 0.0064.
Values may be sent and summed in bfloat16 or wider, within the bound.
No kernel may reach another device: no remote copies, remote signals or barrier semaphores. Data moves between devices by JAX's collectives and lax.ppermute only.
A program may use at most 64 MiB of HBM per device.

v0:
```python
import jax
import jax.numpy as jnp
from jax import lax
from jax.sharding import PartitionSpec as P

SHARDS = 4


def silu_parts(preact):
    sigmoid_of = jax.nn.sigmoid(preact)
    activated = preact * sigmoid_of
    derivative = sigmoid_of * (1.0 + preact * (1.0 - sigmoid_of))
    return (activated, derivative)


def contract_last(first_op, second_op):
    return lax.dot_general(
        first_op, second_op, (((1,), (1,)), ((), ())), preferred_element_type=jnp.float32
    )


def contract_first(first_op, second_op):
    return lax.dot_general(
        first_op, second_op, (((0,), (0,)), ((), ())), preferred_element_type=jnp.float32
    )


def forward_rows(rows_x, gate_w, up_w, down_w):
    pre_gate = contract_last(rows_x, gate_w)
    pre_up = contract_last(rows_x, up_w)
    activated, derivative = silu_parts(pre_gate)
    hidden = (activated * pre_up).astype(jnp.bfloat16)
    return jnp.dot(hidden, down_w, preferred_element_type=jnp.float32).astype(jnp.bfloat16)


def backward_rows(rows_x, rows_do, gate_w, up_w, down_w):
    pre_gate = contract_last(rows_x, gate_w)
    pre_up = contract_last(rows_x, up_w)
    activated, derivative = silu_parts(pre_gate)
    hidden = (activated * pre_up).astype(jnp.bfloat16)
    d_hidden = contract_last(rows_do, down_w)
    d_pre_gate = (d_hidden * pre_up * derivative).astype(jnp.bfloat16)
    d_pre_up = (d_hidden * activated).astype(jnp.bfloat16)
    part_grad = (
        jnp.dot(d_pre_gate, gate_w, preferred_element_type=jnp.float32)
        + jnp.dot(d_pre_up, up_w, preferred_element_type=jnp.float32)
    ).astype(jnp.bfloat16)
    gradients = (
        contract_first(d_pre_gate, rows_x),
        contract_first(d_pre_up, rows_x),
        contract_first(hidden, rows_do),
    )
    return (part_grad, gradients)


def per_device(tokens, cotangent, expert_ids, gate_weights, w_gate, w_up, w_down):
    full_x, full_dy = (
        lax.all_gather(tokens, "expert", axis=1, tiled=True),
        lax.all_gather(cotangent, "expert", axis=1, tiled=True),
    )
    dp_count = lax.axis_size("dp")
    column_count = lax.axis_size("expert")
    column = lax.axis_index("expert")
    tok_count, chosen = expert_ids.shape
    features = full_x.shape[1]
    experts_all = dp_count * column_count // SHARDS
    capacity = min(tok_count, max(2, 2 * tok_count * chosen // experts_all))
    per_row = column_count // SHARDS
    assigned = tok_count * chosen
    flat_ids = expert_ids.reshape(-1)
    flat_gates = gate_weights.reshape(-1)
    owned_here = flat_ids % per_row == column // SHARDS
    target_row = flat_ids // per_row
    onehot = (
        (target_row[:, None] == jnp.arange(dp_count, dtype=jnp.int32)[None, :])
        & owned_here[:, None]
    ).astype(jnp.int32)
    rank_of = jnp.sum((jnp.cumsum(onehot, axis=0) - 1) * onehot, axis=1)
    target = jnp.where(owned_here, target_row * capacity + rank_of, dp_count * capacity)
    slot_src = (
        jnp.full((dp_count * capacity,), assigned, jnp.int32)
        .at[target]
        .set(jnp.arange(assigned, dtype=jnp.int32), mode="drop")
    )
    filled = slot_src < assigned
    safe_index = jnp.where(filled, slot_src, 0)
    slot_token = safe_index // chosen
    slot_gate = jnp.where(filled, flat_gates[safe_index], 0.0)
    slot_dy = full_dy[slot_token].astype(jnp.float32)
    send_x = jnp.where(filled[:, None], full_x[slot_token], jnp.zeros((), full_x.dtype)).reshape(
        dp_count, capacity, features
    )
    send_do = (
        (slot_gate[:, None] * slot_dy).astype(jnp.bfloat16).reshape(dp_count, capacity, features)
    )
    weights = (w_gate[0], w_up[0], w_down[0])
    recv_x = lax.all_to_all(send_x, "dp", split_axis=0, concat_axis=0, tiled=True)
    rows_x = recv_x.reshape(dp_count * capacity, features)
    expert_out = forward_rows(rows_x, *weights)
    back_out = lax.all_to_all(
        expert_out.reshape(dp_count, capacity, features),
        "dp",
        split_axis=0,
        concat_axis=0,
        tiled=True,
    )
    recv_do = lax.all_to_all(send_do, "dp", split_axis=0, concat_axis=0, tiled=True)
    rows_do = recv_do.reshape(dp_count * capacity, features)
    part_grad, gradients = backward_rows(rows_x, rows_do, *weights)
    back_grad = lax.all_to_all(
        part_grad.reshape(dp_count, capacity, features),
        "dp",
        split_axis=0,
        concat_axis=0,
        tiled=True,
    )
    width_now = back_out.shape[2]
    out_float = back_out.reshape(dp_count * capacity, width_now).astype(jnp.float32)
    grad_float = back_grad.reshape(dp_count * capacity, width_now).astype(jnp.float32)
    out_part = (
        jnp.zeros((tok_count, width_now), jnp.float32)
        .at[slot_token]
        .add(slot_gate[:, None] * out_float)
    )
    grad_part = jnp.zeros((tok_count, width_now), jnp.float32).at[slot_token].add(grad_float)
    gate_terms = jnp.sum(slot_dy * out_float, axis=1)
    gate_part = (
        jnp.zeros((assigned,), jnp.float32)
        .at[slot_src]
        .add(gate_terms, mode="drop")
        .reshape(tok_count, chosen)
    )
    out_slice, grad_slice = (
        lax.psum_scatter(out_part, "expert", scatter_dimension=1, tiled=True),
        lax.psum_scatter(grad_part, "expert", scatter_dimension=1, tiled=True),
    )
    grad_gates = lax.psum(gate_part, "expert")
    return (
        out_slice.astype(jnp.bfloat16),
        grad_slice.astype(jnp.bfloat16),
        grad_gates,
        gradients[0].astype(jnp.bfloat16)[None],
        gradients[1].astype(jnp.bfloat16)[None],
        gradients[2].astype(jnp.bfloat16)[None],
    )


def solution(mesh):
    placed = (
        P("dp", "expert"),
        P("dp", "expert"),
        P("dp", None),
        P("dp", None),
        P(("dp", "expert"), None, None),
        P(("dp", "expert"), None, None),
        P(("dp", "expert"), None, None),
    )
    return jax.shard_map(
        per_device,
        mesh=mesh,
        in_specs=placed,
        out_specs=(
            P("dp", "expert"),
            P("dp", "expert"),
            P("dp", None),
            P(("dp", "expert"), None, None),
            P(("dp", "expert"), None, None),
            P(("dp", "expert"), None, None),
        ),
        check_vma=False,
    )
```

profile of v0, /device:TPU:2, one launch (start us, length us, event | category | flops | bytes accessed | tf_op | source)
XLA Modules:
  0.0 339.8 jit_solution(6316037226412424405)
XLA Ops:
  8.4 9.0 %reduce-window.6 = s32[32,8,128]{2,1,0:T(8,128)S(1)} reduce-window(s32[32,8,128]{2,1,0:T(8,128)S(1)} %fusion.25, s32[]{:T(128)} %constant.66.clone.1), window={size=1x1x128 pad=0_0x0_0x127_0}, to_apply=%region_0.1 | reduce-window | flops 4161536 | bytes 262148 | tf_op jit(solution)/shard_map/reduce-window
  18.0 4.3 %scatter_custom_fusion = s32[512]{0:T(512)S(1)} fusion(s32[1024]{0:T(1024)S(1)} %bitcast.72, s32[1024]{0:T(1024)S(1)} %iota.11, s32[]{:T(128)} %constant.65.clone.1), kind=kCustom, calls=%fused_computation.91 | custom fusion | bytes 2052 | tf_op jit(solution)/shard_map/scatter | solution.py:83
  22.5 38.8 %all_gather.6 = bf16[128,2048]{1,0:T(8,128)(2,1)S(1)} all-gather(bf16[128,128]{1,0:T(8,128)(2,1)} %param.7), channel_id=1, replica_groups=mesh['dp'=32,'expert'=16] {'expert'}, dimensions={1}, use_global_device_ids=true | all-gather | bytes 557056 | tf_op jit(solution)/shard_map/all_gather | solution.py:58
  65.3 7.8 %all-to-all-start = ((bf16[32,16,2048]{2,1,0:T(8,128)(2,1)}), bf16[32,16,2048]{2,1,0:T(8,128)(2,1)}, u32[]{:S(2)}, u32[]{:S(2)}) async-start(bf16[32,16,2048]{2,1,0:T(8,128)(2,1)} %broadcast_select_fusion), calls=%async_computation | async-start | bytes 4194304 | tf_op jit(solution)/shard_map/all_to_all | solution.py:97
  75.7 28.7 %all_gather.7 = bf16[128,2048]{1,0:T(8,128)(2,1)S(1)} all-gather(bf16[128,128]{1,0:T(8,128)(2,1)S(1)} %copy-done.2), channel_id=1, replica_groups=mesh['dp'=32,'expert'=16] {'expert'}, dimensions={1}, use_global_device_ids=true | all-gather | bytes 557056 | tf_op jit(solution)/shard_map/all_gather | solution.py:59
  108.6 7.4 %all-to-all-start.2 = ((bf16[32,16,2048]{2,1,0:T(8,128)(2,1)}), bf16[32,16,2048]{2,1,0:T(8,128)(2,1)}, u32[]{:S(2)}, u32[]{:S(2)}) async-start(bf16[32,16,2048]{2,1,0:T(8,128)(2,1)} %fusion), calls=%async_computation.3 | async-start | bytes 4194304 | tf_op jit(solution)/shard_map/all_to_all | solution.py:107
  116.1 3.4 %fusion.11 = f32[512,192]{0,1:T(8,128)} fusion(bf16[512,2048]{1,0:T(8,128)(2,1)} %bitcast.5, bf16[1,192,2048]{2,1,0:T(8,128)(2,1)} %param.12), kind=kOutput, calls=%fused_computation.27 | convolution fusion | flops 402653184 | bytes 3276800 | tf_op jit(solution)/shard_map/dot_general | solution.py:17
  119.5 3.2 fusion.15
  122.7 19.4 %all-to-all-done.2 = bf16[32,16,2048]{2,1,0:T(8,128)(2,1)} async-done(((bf16[32,16,2048]{2,1,0:T(8,128)(2,1)}), bf16[32,16,2048]{2,1,0:T(8,128)(2,1)}, u32[]{:S(2)}, u32[]{:S(2)}) %all-to-all-start.2) | async-done | bytes 2097184 | tf_op jit(solution)/shard_map/all_to_all | solution.py:107
  142.1 2.7 multiply_convert_fusion
  146.8 7.6 %all-to-all-start.1 = ((bf16[32,16,2048]{2,1,0:T(8,128)(2,1)}), bf16[32,16,2048]{2,1,0:T(8,128)(2,1)}, u32[]{:S(2)}, u32[]{:S(2)}) async-start(bf16[32,16,2048]{2,1,0:T(8,128)(2,1)} %bitcast.67), calls=%async_computation.1 | async-start | bytes 4194304 | tf_op jit(solution)/shard_map/all_to_all | solution.py:100
  154.7 3.8 %fusion.13 = f32[512,2048]{1,0:T(8,128)} fusion(bf16[512,192]{0,1:T(8,128)(2,1)S(1)} %get-tuple-element.15, bf16[1,192,2048]{2,1,0:T(8,128)(2,1)} %param.11), kind=kOutput, calls=%fused_computation.29 | convolution fusion | flops 402653184 | bytes 5177344 | tf_op jit(solution)/shard_map/dot_general | solution.py:45
  158.5 22.0 %all-to-all-done.1 = bf16[32,16,2048]{2,1,0:T(8,128)(2,1)} async-done(((bf16[32,16,2048]{2,1,0:T(8,128)(2,1)}), bf16[32,16,2048]{2,1,0:T(8,128)(2,1)}, u32[]{:S(2)}, u32[]{:S(2)}) %all-to-all-start.1) | async-done | bytes 2097184 | tf_op jit(solution)/shard_map/all_to_all | solution.py:100
  180.4 3.9 %bitcast_multiply_fusion = f32[512,2048]{1,0:T(8,128)} fusion(f32[512]{0:T(512)S(1)} %broadcast_select_fusion.1, bf16[32,16,2048]{2,1,0:T(8,128)(2,1)} %all-to-all-done.1), kind=kLoop, calls=%fused_computation.13 | loop fusion | flops 2097152 | bytes 6293504 | tf_op jit(solution)/shard_map/mul | solution.py:123
  184.3 9.4 %scatter_custom_fusion.1 = f32[128,2048]{1,0:T(8,128)} fusion(s32[512]{0:T(512)S(1)} %get-tuple-element.18, f32[512,2048]{1,0:T(8,128)} %bitcast_multiply_fusion, f32[]{:T(128)} %constant.64.clone.1), kind=kCustom, calls=%fused_computation.34 | custom fusion | flops 1048576 | bytes 1049088 | tf_op jit(solution)/shard_map/scatter-add | solution.py:123
  193.8 3.2 add_convert_fusion
  197.0 32.4 %all_to_all.20 = bf16[32,16,2048]{2,1,0:T(8,128)(2,1)} all-to-all(bf16[32,16,2048]{2,1,0:T(8,128)(2,1)S(1)} %bitcast.66), channel_id=1, replica_groups=mesh['dp'=32,'expert'=16] {'dp'}, dimensions={0} | all-to-all | bytes 4194304 | tf_op jit(solution)/shard_map/all_to_all | solution.py:110
  229.4 9.1 %scatter_custom_fusion.2 = f32[128,2048]{1,0:T(8,128)} fusion(s32[512]{0:T(512)S(1)} %get-tuple-element.18, bf16[512,2048]{1,0:T(8,128)(2,1)} %bitcast.68, f32[]{:T(128)} %constant.64.clone.1), kind=kCustom, calls=%fused_computation.11 | custom fusion | flops 2097152 | bytes 3145732 | tf_op jit(solution)/shard_map/scatter-add | solution.py:125
  238.6 3.1 fusion.6
  241.6 3.1 fusion.5
  244.7 3.1 fusion.4
  250.0 3.5 %scatter_custom_fusion.3 = f32[1024]{0:T(1024)S(1)} fusion(s32[512]{0:T(512)S(1)} %get-tuple-element.17, f32[512]{0:T(512)S(1)} %reshape.293, f32[]{:T(128)} %constant.64.clone.1), kind=kCustom, calls=%fused_computation.85 | custom fusion | flops 512 | bytes 4100 | tf_op jit(solution)/shard_map/scatter-add | solution.py:130
  253.6 54.9 %psum.7 = f32[128,8]{1,0:T(8,128)S(1)} all-reduce(f32[128,8]{1,0:T(8,128)S(1)} %reshape.237), channel_id=1, replica_groups=mesh['dp'=32,'expert'=16] {'expert'}, use_global_device_ids=true, to_apply=%region_10.11 | all-reduce | flops 1024 | bytes 8192 | tf_op jit(solution)/shard_map/psum | solution.py:137
  310.6 20.9 %reduce-scatter.5.cloned.1.call-done = f32[128,128]{1,0:T(8,128)} async-done(((f32[128,2048]{1,0:T(8,128)}), f32[128,128]{1,0:T(8,128)}) %reduce-scatter.5.cloned.1.call-update) | async-done | bytes 65552 | tf_op jit(solution)/shard_map/reduce_scatter | solution.py:135
  (53 shorter events, 20.9 us)
Async XLA Ops:
  7.2 134.9 %copy-start = (bf16[1,192,2048]{2,1,0:T(8,128)(2,1)S(1)}, bf16[1,192,2048]{2,1,0:T(8,128)(2,1)}, u32[]{:S(2)}) copy-start(bf16[1,192,2048]{2,1,0:T(8,128)(2,1)} %param.13) | copy-start | bytes 2359300
  65.3 7.8 %copy-start.3 = (f32[128,8]{0,1:T(8,128)S(1)}, f32[128,8]{0,1:T(8,128)}, u32[]{:S(2)}) copy-start(f32[128,8]{0,1:T(8,128)} %param.10) | copy-start | bytes 12292
  65.3 43.3 %all-to-all-start = ((bf16[32,16,2048]{2,1,0:T(8,128)(2,1)}), bf16[32,16,2048]{2,1,0:T(8,128)(2,1)}, u32[]{:S(2)}, u32[]{:S(2)}) async-start(bf16[32,16,2048]{2,1,0:T(8,128)(2,1)} %broadcast_select_fusion), calls=%async_computation | async-start | bytes 4194304 | tf_op jit(solution)/shard_map/all_to_all | solution.py:97
  73.1 2.6 copy-start.2
  108.6 33.4 %all-to-all-start.2 = ((bf16[32,16,2048]{2,1,0:T(8,128)(2,1)}), bf16[32,16,2048]{2,1,0:T(8,128)(2,1)}, u32[]{:S(2)}, u32[]{:S(2)}) async-start(bf16[32,16,2048]{2,1,0:T(8,128)(2,1)} %fusion), calls=%async_computation.3 | async-start | bytes 4194304 | tf_op jit(solution)/shard_map/all_to_all | solution.py:107
  116.1 3.4 %copy-start.1 = (bf16[1,192,2048]{2,1,0:T(8,128)(2,1)S(1)}, bf16[1,192,2048]{2,1,0:T(8,128)(2,1)}, u32[]{:S(2)}) copy-start(bf16[1,192,2048]{2,1,0:T(8,128)(2,1)} %param.11) | copy-start | bytes 2359300
  146.8 33.6 %all-to-all-start.1 = ((bf16[32,16,2048]{2,1,0:T(8,128)(2,1)}), bf16[32,16,2048]{2,1,0:T(8,128)(2,1)}, u32[]{:S(2)}, u32[]{:S(2)}) async-start(bf16[32,16,2048]{2,1,0:T(8,128)(2,1)} %bitcast.67), calls=%async_computation.1 | async-start | bytes 4194304 | tf_op jit(solution)/shard_map/all_to_all | solution.py:100
  154.4 154.7 %reduce-scatter.3.cloned.1.call-start = ((), (), s32[]{:S(2)}) async-start(), calls=%async_computation.6 | async-start | bytes 1114112 | tf_op jit(solution)/shard_map/reduce_scatter | solution.py:134
  193.8 137.7 %reduce-scatter.5.cloned.1.call-start = ((), (), s32[]{:S(2)}) async-start(), calls=%async_computation.7 | async-start | bytes 1114112 | tf_op jit(solution)/shard_map/reduce_scatter | solution.py:135
Sparse Core Ops, SparseCore 0:
  193.9 66.0 reduce-scatter.2
  263.1 68.3 reduce-scatter.4
where the time goes:
time: 341 us; the launch traced here: 340 us
  blocking collectives  155 us (45%)
  waiting for transfers between devices  62.3 us (18%)
  other arithmetic  43.6 us (13%)
  matrix products  27.6 us (8%)
  starting transfers between devices  23.1 us (7%)
  between operations  14.3 us (4%)
  local copies, waits for them, and re-layouts  14.1 us (4%)
    psum x1, blocking collectives, per_device(): grad_gates = lax.psum(gate_part, 'expert')  54.9 us
    all_gather x1, blocking collectives, per_device(): lax.all_gather(tokens, 'expert', axis=1, tiled=True)  38.8 us
    all_to_all x1, blocking collectives, per_device(): lax.all_to_all(part_grad.reshape(dp_count, capacity, features), 'dp', spl...  32.4 us
    all_gather x1, blocking collectives, per_device(): lax.all_gather(cotangent, 'expert', axis=1, tiled=True)  28.7 us
    all_to_all x1, waiting for transfers between devices, per_device(): lax.all_to_all(expert_out.reshape(dp_count, capacity, features), 'dp', sp...  22 us
    reduce_scatter x1, waiting for transfers between devices, per_device(): lax.psum_scatter(grad_part, 'expert', scatter_dimension=1, tiled=True)  20.9 us
    all_to_all x1, waiting for transfers between devices, per_device(): lax.all_to_all(send_do, 'dp', split_axis=0, concat_axis=0, tiled=True)  19.4 us
    scatter-add x1, other arithmetic, per_device(): out_part = jnp.zeros((tok_count, width_now), jnp.float32).at[slot_token]....  9.44 us
  transfers between devices with their start and end apart: 5, of which 3 were waited for; matrix products, arithmetic and copies ran while one was open for 14% of the time, Pallas kernels for 0%

commit v1 on v0

--- a/solution.py
+++ b/solution.py
@@ -56,7 +56,12 @@
 def per_device(tokens, cotangent, expert_ids, gate_weights, w_gate, w_up, w_down):
     full_x, full_dy = (
         lax.all_gather(tokens, "expert", axis=1, tiled=True),
-        lax.all_gather(cotangent, "expert", axis=1, tiled=True),
+        jnp.concatenate(
+            lax.all_to_all(
+                jnp.stack([cotangent for _ in range(lax.psum(1, "expert"))], axis=0), "expert", 0, 0
+            ),
+            axis=1,
+        ),
     )
     dp_count = lax.axis_size("dp")
     column_count = lax.axis_size("expert")

time: 341 us -> 349 us (1.023)
  the two profiles are of different devices: /device:TPU:2 before, /device:TPU:10 now
where the time goes in v1:
time: 349 us; the launch traced here: 347 us
  blocking collectives  123 us (35%)
  waiting for transfers between devices  83.5 us (24%)
  other arithmetic  43.6 us (12%)
  starting transfers between devices  38.9 us (11%)
  matrix products  27.6 us (8%)
  local copies, waits for them, and re-layouts  16.9 us (5%)
  between operations  14.3 us (4%)
    psum x1, blocking collectives, per_device(): grad_gates = lax.psum(gate_part, 'expert')  54.1 us
    all_gather x1, blocking collectives, per_device(): lax.all_gather(tokens, 'expert', axis=1, tiled=True)  36 us
    all_to_all x1, blocking collectives, per_device(): lax.all_to_all(part_grad.reshape(dp_count, capacity, features), 'dp', spl...  32.6 us
    reduce_scatter x1, waiting for transfers between devices, per_device(): lax.psum_scatter(grad_part, 'expert', scatter_dimension=1, tiled=True)  24.6 us
    all_to_all x1, waiting for transfers between devices, per_device(): lax.all_to_all(expert_out.reshape(dp_count, capacity, features), 'dp', sp...  21.8 us
    all_to_all x1, waiting for transfers between devices, per_device(): lax.all_to_all(send_do, 'dp', split_axis=0, concat_axis=0, tiled=True)  19.2 us
    all_to_all x1, waiting for transfers between devices, per_device(): lax.all_to_all(send_x, 'dp', split_axis=0, concat_axis=0, tiled=True)  17.9 us
    all_to_all x1, starting transfers between devices, per_device(): lax.all_to_all(jnp.stack([cotangent for _ in range(lax.psum(1, 'expert'))...  15.2 us
  transfers between devices with their start and end apart: 6, of which 4 were waited for; matrix products, arithmetic and copies ran while one was open for 19% of the time, Pallas kernels for 0%

profile of v1, /device:TPU:10, one launch (start us, length us, event | category | flops | bytes accessed | tf_op | source)
XLA Modules:
  0.0 347.5 jit_solution(8821853713130843004)
XLA Ops:
  8.9 15.2 %all-to-all-start.2 = ((bf16[16,128,128]{2,1,0:T(8,128)(2,1)}), bf16[16,128,128]{2,1,0:T(8,128)(2,1)}, u32[]{:S(2)}, u32[]{:S(2)}) async-start(bf16[16,128,128]{2,1,0:T(8,128)(2,1)} %stack.2), calls=%async_computation.3 | async-start | bytes 1048576 | tf_op jit(solution)/shard_map/all_to_all | solution.py:60
  25.4 9.0 %reduce-window.6 = s32[32,8,128]{2,1,0:T(8,128)S(1)} reduce-window(s32[32,8,128]{2,1,0:T(8,128)S(1)} %fusion.25, s32[]{:T(128)} %constant.66.clone.1), window={size=1x1x128 pad=0_0x0_0x127_0}, to_apply=%region_0.1 | reduce-window | flops 4161536 | bytes 262148 | tf_op jit(solution)/shard_map/reduce-window
  34.9 4.3 %scatter_custom_fusion = s32[512]{0:T(512)S(1)} fusion(s32[1024]{0:T(1024)S(1)} %bitcast.78, s32[1024]{0:T(1024)S(1)} %iota.11, s32[]{:T(128)} %constant.65.clone.1), kind=kCustom, calls=%fused_computation.92 | custom fusion | bytes 2052 | tf_op jit(solution)/shard_map/scatter | solution.py:88
  39.4 36.0 %all_gather.3 = bf16[128,2048]{1,0:T(8,128)(2,1)S(1)} all-gather(bf16[128,128]{1,0:T(8,128)(2,1)S(1)} %copy-done.2), channel_id=1, replica_groups=mesh['dp'=32,'expert'=16] {'expert'}, dimensions={1}, use_global_device_ids=true | all-gather | bytes 557056 | tf_op jit(solution)/shard_map/all_gather | solution.py:58
  79.5 7.7 %all-to-all-start = ((bf16[32,16,2048]{2,1,0:T(8,128)(2,1)}), bf16[32,16,2048]{2,1,0:T(8,128)(2,1)}, u32[]{:S(2)}, u32[]{:S(2)}) async-start(bf16[32,16,2048]{2,1,0:T(8,128)(2,1)} %broadcast_select_fusion), calls=%async_computation | async-start | bytes 4194304 | tf_op jit(solution)/shard_map/all_to_all | solution.py:102
  95.1 17.9 %all-to-all-done = bf16[32,16,2048]{2,1,0:T(8,128)(2,1)} async-done(((bf16[32,16,2048]{2,1,0:T(8,128)(2,1)}), bf16[32,16,2048]{2,1,0:T(8,128)(2,1)}, u32[]{:S(2)}, u32[]{:S(2)}) %all-to-all-start) | async-done | bytes 2097184 | tf_op jit(solution)/shard_map/all_to_all | solution.py:102
  113.0 7.8 %all-to-all-start.3 = ((bf16[32,16,2048]{2,1,0:T(8,128)(2,1)}), bf16[32,16,2048]{2,1,0:T(8,128)(2,1)}, u32[]{:S(2)}, u32[]{:S(2)}) async-start(bf16[32,16,2048]{2,1,0:T(8,128)(2,1)} %fusion), calls=%async_computation.4 | async-start | bytes 4194304 | tf_op jit(solution)/shard_map/all_to_all | solution.py:112
  120.8 3.4 fusion.11
  124.3 3.2 fusion.15
  127.4 19.2 %all-to-all-done.3 = bf16[32,16,2048]{2,1,0:T(8,128)(2,1)} async-done(((bf16[32,16,2048]{2,1,0:T(8,128)(2,1)}), bf16[32,16,2048]{2,1,0:T(8,128)(2,1)}, u32[]{:S(2)}, u32[]{:S(2)}) %all-to-all-start.3) | async-done | bytes 2097184 | tf_op jit(solution)/shard_map/all_to_all | solution.py:112
  151.4 7.8 %all-to-all-start.1 = ((bf16[32,16,2048]{2,1,0:T(8,128)(2,1)}), bf16[32,16,2048]{2,1,0:T(8,128)(2,1)}, u32[]{:S(2)}, u32[]{:S(2)}) async-start(bf16[32,16,2048]{2,1,0:T(8,128)(2,1)} %bitcast.73), calls=%async_computation.1 | async-start | bytes 4194304 | tf_op jit(solution)/shard_map/all_to_all | solution.py:105
  159.4 3.8 %fusion.13 = f32[512,2048]{1,0:T(8,128)} fusion(bf16[512,192]{0,1:T(8,128)(2,1)S(1)} %get-tuple-element.21, bf16[1,192,2048]{2,1,0:T(8,128)(2,1)} %param.11), kind=kOutput, calls=%fused_computation.29 | convolution fusion | flops 402653184 | bytes 5177344 | tf_op jit(solution)/shard_map/dot_general | solution.py:45
  163.3 21.8 %all-to-all-done.1 = bf16[32,16,2048]{2,1,0:T(8,128)(2,1)} async-done(((bf16[32,16,2048]{2,1,0:T(8,128)(2,1)}), bf16[32,16,2048]{2,1,0:T(8,128)(2,1)}, u32[]{:S(2)}, u32[]{:S(2)}) %all-to-all-start.1) | async-done | bytes 2097184 | tf_op jit(solution)/shard_map/all_to_all | solution.py:105
  185.0 3.9 %bitcast_multiply_fusion = f32[512,2048]{1,0:T(8,128)} fusion(f32[512]{0:T(512)S(1)} %broadcast_select_fusion.1, bf16[32,16,2048]{2,1,0:T(8,128)(2,1)} %all-to-all-done.1), kind=kLoop, calls=%fused_computation.13 | loop fusion | flops 2097152 | bytes 6293504 | tf_op jit(solution)/shard_map/mul | solution.py:128
  188.9 9.4 %scatter_custom_fusion.1 = f32[128,2048]{1,0:T(8,128)} fusion(s32[512]{0:T(512)S(1)} %get-tuple-element.24, f32[512,2048]{1,0:T(8,128)} %bitcast_multiply_fusion, f32[]{:T(128)} %constant.64.clone.1), kind=kCustom, calls=%fused_computation.35 | custom fusion | flops 1048576 | bytes 1049088 | tf_op jit(solution)/shard_map/scatter-add | solution.py:128
  198.5 3.2 add_convert_fusion
  201.6 32.6 %all_to_all.25 = bf16[32,16,2048]{2,1,0:T(8,128)(2,1)} all-to-all(bf16[32,16,2048]{2,1,0:T(8,128)(2,1)S(1)} %bitcast.72), channel_id=1, replica_groups=mesh['dp'=32,'expert'=16] {'dp'}, dimensions={0} | all-to-all | bytes 4194304 | tf_op jit(solution)/shard_map/all_to_all | solution.py:115
  234.2 9.1 %scatter_custom_fusion.2 = f32[128,2048]{1,0:T(8,128)} fusion(s32[512]{0:T(512)S(1)} %get-tuple-element.24, bf16[512,2048]{1,0:T(8,128)(2,1)} %bitcast.74, f32[]{:T(128)} %constant.64.clone.1), kind=kCustom, calls=%fused_computation.11 | custom fusion | flops 2097152 | bytes 3145732 | tf_op jit(solution)/shard_map/scatter-add | solution.py:130
  243.3 3.1 fusion.6
  246.4 3.1 fusion.5
  249.5 3.1 fusion.4
  254.8 3.5 scatter_custom_fusion.3
  258.4 54.1 %psum.7 = f32[128,8]{1,0:T(8,128)S(1)} all-reduce(f32[128,8]{1,0:T(8,128)S(1)} %reshape.247), channel_id=1, replica_groups=mesh['dp'=32,'expert'=16] {'expert'}, use_global_device_ids=true, to_apply=%region_10.11 | all-reduce | flops 1024 | bytes 8192 | tf_op jit(solution)/shard_map/psum | solution.py:142
  314.6 24.6 %reduce-scatter.5.cloned.1.call-done = f32[128,128]{1,0:T(8,128)} async-done(((f32[128,2048]{1,0:T(8,128)}), f32[128,128]{1,0:T(8,128)}) %reduce-scatter.5.cloned.1.call-update) | async-done | bytes 65552 | tf_op jit(solution)/shard_map/reduce_scatter | solution.py:140
  (56 shorter events, 26.4 us)
Async XLA Ops:
  7.2 139.5 %copy-start = (bf16[1,192,2048]{2,1,0:T(8,128)(2,1)S(1)}, bf16[1,192,2048]{2,1,0:T(8,128)(2,1)}, u32[]{:S(2)}) copy-start(bf16[1,192,2048]{2,1,0:T(8,128)(2,1)} %param.13) | copy-start | bytes 2359300
  7.2 32.2 %copy-start.2 = (bf16[128,128]{1,0:T(8,128)(2,1)S(1)}, bf16[128,128]{1,0:T(8,128)(2,1)}, u32[]{:S(2)}) copy-start(bf16[128,128]{1,0:T(8,128)(2,1)} %param.7) | copy-start | bytes 98308
  8.9 70.6 %all-to-all-start.2 = ((bf16[16,128,128]{2,1,0:T(8,128)(2,1)}), bf16[16,128,128]{2,1,0:T(8,128)(2,1)}, u32[]{:S(2)}, u32[]{:S(2)}) async-start(bf16[16,128,128]{2,1,0:T(8,128)(2,1)} %stack.2), calls=%async_computation.3 | async-start | bytes 1048576 | tf_op jit(solution)/shard_map/all_to_all | solution.py:60
  79.5 7.7 %copy-start.3 = (f32[128,8]{0,1:T(8,128)S(1)}, f32[128,8]{0,1:T(8,128)}, u32[]{:S(2)}) copy-start(f32[128,8]{0,1:T(8,128)} %param.10) | copy-start | bytes 12292
  79.5 33.5 %all-to-all-start = ((bf16[32,16,2048]{2,1,0:T(8,128)(2,1)}), bf16[32,16,2048]{2,1,0:T(8,128)(2,1)}, u32[]{:S(2)}, u32[]{:S(2)}) async-start(bf16[32,16,2048]{2,1,0:T(8,128)(2,1)} %broadcast_select_fusion), calls=%async_computation | async-start | bytes 4194304 | tf_op jit(solution)/shard_map/all_to_all | solution.py:102
  113.0 33.7 %all-to-all-start.3 = ((bf16[32,16,2048]{2,1,0:T(8,128)(2,1)}), bf16[32,16,2048]{2,1,0:T(8,128)(2,1)}, u32[]{:S(2)}, u32[]{:S(2)}) async-start(bf16[32,16,2048]{2,1,0:T(8,128)(2,1)} %fusion), calls=%async_computation.4 | async-start | bytes 4194304 | tf_op jit(solution)/shard_map/all_to_all | solution.py:112
  120.8 3.4 copy-start.1
  151.4 33.6 %all-to-all-start.1 = ((bf16[32,16,2048]{2,1,0:T(8,128)(2,1)}), bf16[32,16,2048]{2,1,0:T(8,128)(2,1)}, u32[]{:S(2)}, u32[]{:S(2)}) async-start(bf16[32,16,2048]{2,1,0:T(8,128)(2,1)} %bitcast.73), calls=%async_computation.1 | async-start | bytes 4194304 | tf_op jit(solution)/shard_map/all_to_all | solution.py:105
  159.2 153.9 %reduce-scatter.3.cloned.1.call-start = ((), (), s32[]{:S(2)}) async-start(), calls=%async_computation.7 | async-start | bytes 1114112 | tf_op jit(solution)/shard_map/reduce_scatter | solution.py:139
  198.4 140.8 %reduce-scatter.5.cloned.1.call-start = ((), (), s32[]{:S(2)}) async-start(), calls=%async_computation.8 | async-start | bytes 1114112 | tf_op jit(solution)/shard_map/reduce_scatter | solution.py:140
Sparse Core Ops, SparseCore 0:
  198.5 69.0 reduce-scatter.2
  270.7 68.4 reduce-scatter.4
